TPU v7x, 128 devices: a whole 4x4x4 slice. The times are simulated.
128 devices in a mesh: gx: 16 (over z, y_hi, core), gy: 8 (over y_lo, x).
Axes of the slice: x: 4, y: 4 (y_hi: 2, y_lo: 2; y = y_hi * 2 + y_lo), z: 4, core: 2. Of those that a mesh axis runs over, the one named last changes fastest.
Arguments:
- features: bfloat16 [16, 8, 32, 64, 256], P('gx', 'gy'), may hold values from -6 to 6
- weights: bfloat16 [27, 256, 256], replicated, may hold values from -0.078125 to 0.078125
- cotangent: bfloat16 [16, 8, 32, 64, 256], P('gx', 'gy'), may hold values from -6 to 6
- send_lists: int32 [16, 8, 8, 8], P('gx', 'gy'), may hold values from 0 to 31, as said below
- block_offset: int32 [16, 8, 108], P('gx', 'gy'), may hold values from 0 to 26, as said below
- block_input: int32 [16, 8, 108, 8], P('gx', 'gy'), may hold values from 0 to 95
- block_output: int32 [16, 8, 108, 8], P('gx', 'gy'), may hold values from 0 to 32, as said below
- block_count: int32 [16, 8], P('gx', 'gy'), may hold values from 1 to 108, as said below
Outputs:
- out_features: bfloat16 [16, 8, 32, 64, 256], P('gx', 'gy')
- feat_grad: bfloat16 [16, 8, 32, 64, 256], P('gx', 'gy')
- weight_grad: float32 [27, 256, 256], replicated
Inputs may be any that keep to these rules, and one draw needn't show every extreme that they name: `send_lists`: each of a device's 8 lists names 8 different tiles that the device holds. `block_offset`: 0 in blocks past block_count. `block_output`: 32 marks an unused pair; a device's used pairs of one offset name different tiles; the used blocks come first, grouped by offset, and blocks past block_count hold only unused pairs. `block_count`: some device uses all 108 blocks.
All inputs are finite; a program needn't handle non-finite values.
Results may differ from a plain program's by a relative error of at most 0.0029.
Values may be sent and summed in bfloat16 or wider, within the bound.
A program may use at most 128 MiB of HBM per device.

v0:
```python
import math
import jax
import jax.numpy as jnp
from jax import lax
from jax.sharding import PartitionSpec as P

DIRECTIONS = ((-1, -1), (-1, 0), (-1, 1), (0, -1), (0, 1), (1, -1), (1, 0), (1, 1))


def passed_along(x, axis, by):
    size = lax.axis_size(axis)
    pairs = [(i, i + by) for i in range(size) if 0 <= i + by < size]
    return lax.ppermute(x, axis, pairs)


def travel(packet, step_x, step_y):
    moved = packet
    if step_x != 0:
        moved = passed_along(moved, "gx", step_x)
    if step_y != 0:
        moved = passed_along(moved, "gy", step_y)
    return moved


def travel_back(packet, step_x, step_y):
    moved = packet
    if step_y != 0:
        moved = passed_along(moved.astype(jnp.bfloat16), "gy", -step_y).astype(moved.dtype)
    if step_x != 0:
        moved = passed_along(moved.astype(jnp.bfloat16), "gx", -step_x).astype(moved.dtype)
    return moved


def shards(
    features, weights, cotangent, send_lists, block_offset, block_input, block_output, block_count
):
    tiles = features[0, 0]
    tile_slots, voxels, channels = tiles.shape
    lists = send_lists[0, 0]
    halo_size = lists.shape[1]
    packets = tiles[lists]
    halo = jnp.stack(
        [travel(packets[which], pair[0], pair[1]) for which, pair in enumerate(DIRECTIONS)]
    )
    extended = jnp.concatenate([tiles, halo.reshape(8 * halo_size, voxels, channels)], axis=0)
    per_turn = 8
    block_slots = block_offset.shape[2]
    block_rows = block_input.shape[3]
    padded_slots = -(-block_slots // per_turn) * per_turn
    extra = padded_slots - block_slots
    used_blocks = block_count[0, 0]
    live = jnp.arange(padded_slots) < used_blocks
    offsets = jnp.pad(block_offset[0, 0], (0, extra))
    inputs = jnp.pad(block_input[0, 0], ((0, extra), (0, 0)))
    outputs = jnp.pad(block_output[0, 0], ((0, extra), (0, 0)), constant_values=tile_slots)
    outputs = jnp.where(live[:, None], outputs, tile_slots)
    turn_count = (used_blocks + per_turn - 1) // per_turn

    def slices(turn):
        start = turn * per_turn
        return (
            lax.dynamic_slice_in_dim(offsets, start, per_turn),
            lax.dynamic_slice_in_dim(inputs, start, per_turn),
            lax.dynamic_slice_in_dim(outputs, start, per_turn),
        )

    def forward_turn(turn, accum):
        turn_offsets, turn_inputs, turn_outputs = slices(turn)
        gathered = extended[turn_inputs.reshape(-1)].reshape(
            per_turn, block_rows * voxels, channels
        )
        product = jnp.einsum(
            "grc,gcd->grd", gathered, weights[turn_offsets], preferred_element_type=jnp.float32
        )
        return accum.at[turn_outputs.reshape(-1)].add(
            product.reshape(per_turn * block_rows, voxels, channels), mode="drop"
        )

    pre = lax.fori_loop(
        0, turn_count, forward_turn, jnp.zeros((tile_slots, voxels, channels), jnp.float32)
    )
    sigma = jax.nn.sigmoid(pre)
    out_features = (tiles.astype(jnp.float32) + pre * sigma).astype(jnp.bfloat16)
    incoming = cotangent[0, 0].astype(jnp.float32)
    pre_grad = (incoming * sigma * (1.0 + pre * (1.0 - sigma))).astype(jnp.bfloat16)
    padded_grad = jnp.concatenate(
        [pre_grad, jnp.zeros((1, voxels, channels), jnp.bfloat16)], axis=0
    )

    def backward_turn(turn, carry):
        ext_grad, weight_part = carry
        turn_offsets, turn_inputs, turn_outputs = slices(turn)
        gathered = extended[turn_inputs.reshape(-1)].reshape(
            per_turn, block_rows * voxels, channels
        )
        grads = padded_grad[turn_outputs.reshape(-1)].reshape(
            per_turn, block_rows * voxels, channels
        )
        mats = weights[turn_offsets]
        back = jnp.einsum("grd,gcd->grc", grads, mats, preferred_element_type=jnp.float32)
        ext_grad = ext_grad.at[turn_inputs.reshape(-1)].add(
            back.reshape(per_turn * block_rows, voxels, channels)
        )
        terms = jnp.einsum("grc,grd->gcd", gathered, grads, preferred_element_type=jnp.float32)
        weight_part = weight_part.at[turn_offsets].add(terms)
        return (ext_grad, weight_part)

    start = (
        jnp.zeros((tile_slots + 8 * halo_size, voxels, channels), jnp.float32),
        jnp.zeros(weights.shape, jnp.float32),
    )
    ext_grad, weight_part = lax.fori_loop(0, turn_count, backward_turn, start)
    adjoints = ext_grad[tile_slots:].reshape(8, halo_size, voxels, channels)
    returned = jnp.stack(
        [travel_back(adjoints[which], pair[0], pair[1]) for which, pair in enumerate(DIRECTIONS)]
    )
    feat_sum = incoming + ext_grad[:tile_slots]
    feat_sum = feat_sum.at[lists.reshape(-1)].add(returned.reshape(8 * halo_size, voxels, channels))
    feat_grad = feat_sum.astype(jnp.bfloat16)
    weight_total = lax.psum(weight_part, ("gx", "gy"))
    device_total = lax.axis_size("gx") * lax.axis_size("gy")
    weight_grad = weight_total / math.sqrt(voxels * tile_slots * device_total)
    return (out_features[None, None], feat_grad[None, None], weight_grad)


def solution(mesh):
    in_specs = (
        P("gx", "gy", None, None, None),
        P(),
        P("gx", "gy", None, None, None),
        P("gx", "gy", None, None),
        P("gx", "gy", None),
        P("gx", "gy", None, None),
        P("gx", "gy", None, None),
        P("gx", "gy"),
    )
    out_specs = (P("gx", "gy", None, None, None), P("gx", "gy", None, None, None), P())
    return jax.shard_map(shards, mesh=mesh, in_specs=in_specs, out_specs=out_specs, check_vma=False)
```

profile of v0, /device:TPU:1, one launch (start us, length us, event | category | flops | bytes accessed | tf_op | source)
XLA Modules:
  0.0 1024.6 jit_solution(5015731274001047856)
XLA Ops:
  19.4 5.1 collective-permute-start.7
  45.5 5.5 collective-permute-start.11
  54.7 5.9 collective-permute-done.9
  62.8 279.6 %while.22 = (s32[]{:T(128)}, f32[32,64,256]{2,1,0:T(8,128)S(1)}, s32[]{:T(128)}, s32[112,8]{1,0:T(8,128)S(1)}, s32[112,8]{1,0:T(8,128)S(1)}, /*index=5*/bf16[96,...) while((s32[]{:T(128)}, f32[32,64,256]{2,1,0:T(8,128)S(1)}, ...), condition=%wide.region_2.3_spmd, body=%wide.region_0.2_spmd.sunk | while | flops 537921920 | bytes 26226740 | solution.py:79
  74.0 8.8 scatter_fusion
  94.0 8.8 scatter_fusion
  113.9 8.8 scatter_fusion
  133.9 8.8 scatter_fusion
  153.9 8.8 scatter_fusion
  173.8 8.8 scatter_fusion
  193.8 8.8 scatter_fusion
  213.8 8.8 scatter_fusion
  233.7 8.8 scatter_fusion
  253.7 8.8 scatter_fusion
  273.7 8.8 scatter_fusion
  293.7 8.8 scatter_fusion
  313.6 8.8 scatter_fusion
  333.6 8.8 scatter_fusion
  353.4 480.4 %while.23 = (s32[]{:T(128)}, f32[96,64,256]{2,1,0:T(8,128)}, f32[27,256,256]{2,1,0:T(8,128)}, s32[]{:T(128)}, s32[112,8]{1,0:T(8,128)S(1)}, /*index=5*/s32[112,8...) while((s32[]{:T(128)}, f32[96,64,256]{2,1,0:T(8,128)}, ...), condition=%wide.region_6.7_spmd, body=%wide.region_3.6_spmd.sunk | while | flops 1075318144 | bytes 43008608 | solution.py:112
  361.9 13.5 %scatter_fusion.1 = f32[96,64,256]{2,1,0:T(8,128)} fusion(f32[96,64,256]{2,1,0:T(8,128)} %get-tuple-element.332, s32[64]{0:T(128)S(1)} %fusion.41, f32[64,64,256]{2,1,0:T(8,128)} %bitcast.112), kind=kCustom, calls=%fused_computation.7.clone.1 | custom fusion | flops 1048576 | bytes 12583168 | tf_op jit(solution)/shard_map/while/body/scatter-add | solution.py:101
  383.0 4.6 scatter_fusion.2
  396.0 13.5 %scatter_fusion.1 = f32[96,64,256]{2,1,0:T(8,128)} fusion(f32[96,64,256]{2,1,0:T(8,128)} %get-tuple-element.332, s32[64]{0:T(128)S(1)} %fusion.41, f32[64,64,256]{2,1,0:T(8,128)} %bitcast.112), kind=kCustom, calls=%fused_computation.7.clone.1 | custom fusion | flops 1048576 | bytes 12583168 | tf_op jit(solution)/shard_map/while/body/scatter-add | solution.py:101
  417.2 4.8 scatter_fusion.2
  430.4 13.5 %scatter_fusion.1 = f32[96,64,256]{2,1,0:T(8,128)} fusion(f32[96,64,256]{2,1,0:T(8,128)} %get-tuple-element.332, s32[64]{0:T(128)S(1)} %fusion.41, f32[64,64,256]{2,1,0:T(8,128)} %bitcast.112), kind=kCustom, calls=%fused_computation.7.clone.1 | custom fusion | flops 1048576 | bytes 12583168 | tf_op jit(solution)/shard_map/while/body/scatter-add | solution.py:101
  451.5 4.8 scatter_fusion.2
  464.7 13.5 %scatter_fusion.1 = f32[96,64,256]{2,1,0:T(8,128)} fusion(f32[96,64,256]{2,1,0:T(8,128)} %get-tuple-element.332, s32[64]{0:T(128)S(1)} %fusion.41, f32[64,64,256]{2,1,0:T(8,128)} %bitcast.112), kind=kCustom, calls=%fused_computation.7.clone.1 | custom fusion | flops 1048576 | bytes 12583168 | tf_op jit(solution)/shard_map/while/body/scatter-add | solution.py:101
  485.8 4.6 scatter_fusion.2
  498.9 13.4 %scatter_fusion.1 = f32[96,64,256]{2,1,0:T(8,128)} fusion(f32[96,64,256]{2,1,0:T(8,128)} %get-tuple-element.332, s32[64]{0:T(128)S(1)} %fusion.41, f32[64,64,256]{2,1,0:T(8,128)} %bitcast.112), kind=kCustom, calls=%fused_computation.7.clone.1 | custom fusion | flops 1048576 | bytes 12583168 | tf_op jit(solution)/shard_map/while/body/scatter-add | solution.py:101
  533.0 13.4 %scatter_fusion.1 = f32[96,64,256]{2,1,0:T(8,128)} fusion(f32[96,64,256]{2,1,0:T(8,128)} %get-tuple-element.332, s32[64]{0:T(128)S(1)} %fusion.41, f32[64,64,256]{2,1,0:T(8,128)} %bitcast.112), kind=kCustom, calls=%fused_computation.7.clone.1 | custom fusion | flops 1048576 | bytes 12583168 | tf_op jit(solution)/shard_map/while/body/scatter-add | solution.py:101
  554.0 4.7 scatter_fusion.2
  567.1 13.5 %scatter_fusion.1 = f32[96,64,256]{2,1,0:T(8,128)} fusion(f32[96,64,256]{2,1,0:T(8,128)} %get-tuple-element.332, s32[64]{0:T(128)S(1)} %fusion.41, f32[64,64,256]{2,1,0:T(8,128)} %bitcast.112), kind=kCustom, calls=%fused_computation.7.clone.1 | custom fusion | flops 1048576 | bytes 12583168 | tf_op jit(solution)/shard_map/while/body/scatter-add | solution.py:101
  601.3 13.6 %scatter_fusion.1 = f32[96,64,256]{2,1,0:T(8,128)} fusion(f32[96,64,256]{2,1,0:T(8,128)} %get-tuple-element.332, s32[64]{0:T(128)S(1)} %fusion.41, f32[64,64,256]{2,1,0:T(8,128)} %bitcast.112), kind=kCustom, calls=%fused_computation.7.clone.1 | custom fusion | flops 1048576 | bytes 12583168 | tf_op jit(solution)/shard_map/while/body/scatter-add | solution.py:101
  622.5 4.8 scatter_fusion.2
  635.7 13.6 %scatter_fusion.1 = f32[96,64,256]{2,1,0:T(8,128)} fusion(f32[96,64,256]{2,1,0:T(8,128)} %get-tuple-element.332, s32[64]{0:T(128)S(1)} %fusion.41, f32[64,64,256]{2,1,0:T(8,128)} %bitcast.112), kind=kCustom, calls=%fused_computation.7.clone.1 | custom fusion | flops 1048576 | bytes 12583168 | tf_op jit(solution)/shard_map/while/body/scatter-add | solution.py:101
  656.9 4.6 scatter_fusion.2
  670.0 13.6 %scatter_fusion.1 = f32[96,64,256]{2,1,0:T(8,128)} fusion(f32[96,64,256]{2,1,0:T(8,128)} %get-tuple-element.332, s32[64]{0:T(128)S(1)} %fusion.41, f32[64,64,256]{2,1,0:T(8,128)} %bitcast.112), kind=kCustom, calls=%fused_computation.7.clone.1 | custom fusion | flops 1048576 | bytes 12583168 | tf_op jit(solution)/shard_map/while/body/scatter-add | solution.py:101
  704.3 13.6 %scatter_fusion.1 = f32[96,64,256]{2,1,0:T(8,128)} fusion(f32[96,64,256]{2,1,0:T(8,128)} %get-tuple-element.332, s32[64]{0:T(128)S(1)} %fusion.41, f32[64,64,256]{2,1,0:T(8,128)} %bitcast.112), kind=kCustom, calls=%fused_computation.7.clone.1 | custom fusion | flops 1048576 | bytes 12583168 | tf_op jit(solution)/shard_map/while/body/scatter-add | solution.py:101
  725.5 4.7 scatter_fusion.2
  738.6 13.6 %scatter_fusion.1 = f32[96,64,256]{2,1,0:T(8,128)} fusion(f32[96,64,256]{2,1,0:T(8,128)} %get-tuple-element.332, s32[64]{0:T(128)S(1)} %fusion.41, f32[64,64,256]{2,1,0:T(8,128)} %bitcast.112), kind=kCustom, calls=%fused_computation.7.clone.1 | custom fusion | flops 1048576 | bytes 12583168 | tf_op jit(solution)/shard_map/while/body/scatter-add | solution.py:101
  759.8 4.8 scatter_fusion.2
  773.1 13.5 %scatter_fusion.1 = f32[96,64,256]{2,1,0:T(8,128)} fusion(f32[96,64,256]{2,1,0:T(8,128)} %get-tuple-element.332, s32[64]{0:T(128)S(1)} %fusion.41, f32[64,64,256]{2,1,0:T(8,128)} %bitcast.112), kind=kCustom, calls=%fused_computation.7.clone.1 | custom fusion | flops 1048576 | bytes 12583168 | tf_op jit(solution)/shard_map/while/body/scatter-add | solution.py:101
  794.2 4.7 scatter_fusion.2
  807.4 14.2 %scatter_fusion.1 = f32[96,64,256]{2,1,0:T(8,128)} fusion(f32[96,64,256]{2,1,0:T(8,128)} %get-tuple-element.332, s32[64]{0:T(128)S(1)} %fusion.41, f32[64,64,256]{2,1,0:T(8,128)} %bitcast.112), kind=kCustom, calls=%fused_computation.7.clone.1 | custom fusion | flops 1048576 | bytes 12583168 | tf_op jit(solution)/shard_map/while/body/scatter-add | solution.py:101
  862.0 6.8 collective-permute-done.19
  879.9 8.8 collective-permute-done.20
  894.3 8.8 scatter_fusion.3
  904.2 106.8 %all-reduce.6.cloned.1.call-done = f32[27,256,256]{2,1,0:T(8,128)} async-done(((f32[27,256,256]{2,1,0:T(8,128)}), f32[27,256,256]{2,1,0:T(8,128)}) %all-reduce.6.cloned.1.call-update) | async-done | bytes 7077904 | tf_op jit(solution)/shard_map/psum | solution.py:120
  1011.0 6.7 broadcast_multiply_fusion
  (459 shorter events, 493.7 us)
Async XLA Ops:
  7.2 1003.9 %all-reduce.6.cloned.1.call-start = ((), (), s32[]{:S(2)}) async-start(), calls=%async_computation | async-start | bytes 14155776 | tf_op jit(solution)/shard_map/psum | solution.py:120
  9.9 16.6 %copy-start.7 = (s32[1,1,108,8]{2,3,1,0:T(8,128)S(1)}, s32[1,1,108,8]{2,3,1,0:T(8,128)}, u32[]{:S(2)}) copy-start(s32[1,1,108,8]{2,3,1,0:T(8,128)} %param.18) | copy-start | bytes 10372
  9.9 16.8 %copy-start.8 = (s32[1,1,108,8]{2,3,1,0:T(8,128)S(1)}, s32[1,1,108,8]{2,3,1,0:T(8,128)}, u32[]{:S(2)}) copy-start(s32[1,1,108,8]{2,3,1,0:T(8,128)} %param.17) | copy-start | bytes 10372
  9.9 17.0 %copy-start.9 = (s32[1,1,108]{2,1,0:T(1,128)S(1)}, s32[1,1,108]{2,1,0:T(1,128)}, u32[]{:S(2)}) copy-start(s32[1,1,108]{2,1,0:T(1,128)} %param.16) | copy-start | bytes 1300
  11.0 14.2 %collective-permute-start = (bf16[8,64,256]{2,1,0:T(8,128)(2,1)S(1)}, bf16[8,64,256]{2,1,0:T(8,128)(2,1)S(1)}, u32[]{:S(2)}, u32[]{:S(2)}) collective-permute-start(bf16[8,64,256]{2,1,0:T(8,128)(2,1)S(1)} %get-tuple-element.160), channel_id=1, source_target_pairs={{8,0},{16,8},{24,16},{32,24},{40,32},{48,40},{56,48},{64,56},{72,6... | collective-permute-start | bytes 786440 | tf_op jit(solution)/shard_map/ppermute | solution.py:13
  14.2 22.7 %collective-permute-start.2 = (bf16[8,64,256]{2,1,0:T(8,128)(2,1)}, bf16[8,64,256]{2,1,0:T(8,128)(2,1)S(1)}, u32[]{:S(2)}, u32[]{:S(2)}) collective-permute-start(bf16[8,64,256]{2,1,0:T(8,128)(2,1)} %get-tuple-element.159), channel_id=1, source_target_pairs={{8,0},{16,8},{24,16},{32,24},{40,32},{48,40},{56,48},{64,56},{72,6... | collective-permute-start | bytes 786440 | tf_op jit(solution)/shard_map/ppermute | solution.py:13
  16.2 10.7 %collective-permute-start.3 = (bf16[8,64,256]{2,1,0:T(8,128)(2,1)}, bf16[8,64,256]{2,1,0:T(8,128)(2,1)S(1)}, u32[]{:S(2)}, u32[]{:S(2)}) collective-permute-start(bf16[8,64,256]{2,1,0:T(8,128)(2,1)} %get-tuple-element.158), channel_id=1, source_target_pairs={{8,0},{16,8},{24,16},{32,24},{40,32},{48,40},{56,48},{64,56},{72,6... | collective-permute-start | bytes 786440 | tf_op jit(solution)/shard_map/ppermute | solution.py:13
  18.1 32.9 %collective-permute-start.5 = (bf16[8,64,256]{2,1,0:T(8,128)(2,1)S(1)}, bf16[8,64,256]{2,1,0:T(8,128)(2,1)S(1)}, u32[]{:S(2)}, u32[]{:S(2)}) collective-permute-start(bf16[8,64,256]{2,1,0:T(8,128)(2,1)S(1)} %get-tuple-element.157), channel_id=1, source_target_pairs={{1,0},{2,1},{3,2},{4,3},{5,4},{6,5},{7,6},{9,8},{10,9},{11,10},{12... | collective-permute-start | bytes 786440 | tf_op jit(solution)/shard_map/ppermute | solution.py:13
  19.4 20.8 %collective-permute-start.7 = (bf16[8,64,256]{2,1,0:T(8,128)(2,1)S(1)}, bf16[8,64,256]{2,1,0:T(8,128)(2,1)S(1)}, u32[]{:S(2)}, u32[]{:S(2)}) collective-permute-start(bf16[8,64,256]{2,1,0:T(8,128)(2,1)S(1)} %get-tuple-element.155), channel_id=1, source_target_pairs={{0,8},{8,16},{16,24},{24,32},{32,40},{40,48},{48,56},{56,64},{64,7... | collective-permute-start | bytes 786440 | tf_op jit(solution)/shard_map/ppermute | solution.py:13
  25.2 8.0 collective-permute-start.1
  26.9 33.8 %copy-start = (bf16[1,1,32,64,256]{4,3,2,1,0:T(8,128)(2,1)S(1)}, bf16[1,1,32,64,256]{4,3,2,1,0:T(8,128)(2,1)}, u32[]{:S(2)}) copy-start(bf16[1,1,32,64,256]{4,3,2,1,0:T(8,128)(2,1)} %param.12) | copy-start | bytes 3145732
  26.9 17.2 %collective-permute-start.10 = (bf16[8,64,256]{2,1,0:T(8,128)(2,1)S(1)}, bf16[8,64,256]{2,1,0:T(8,128)(2,1)S(1)}, u32[]{:S(2)}, u32[]{:S(2)}) collective-permute-start(bf16[8,64,256]{2,1,0:T(8,128)(2,1)S(1)} %get-tuple-element.153), channel_id=1, source_target_pairs={{0,8},{8,16},{16,24},{24,32},{32,40},{40,48},{48,56},{56,64},{64,7... | collective-permute-start | bytes 786440 | tf_op jit(solution)/shard_map/ppermute | solution.py:13
  33.2 12.2 %collective-permute-start.4 = (bf16[8,64,256]{2,1,0:T(8,128)(2,1)S(1)}, bf16[8,64,256]{2,1,0:T(8,128)(2,1)S(1)}, u32[]{:S(2)}, u32[]{:S(2)}) collective-permute-start(bf16[8,64,256]{2,1,0:T(8,128)(2,1)S(1)} %collective-permute-done.3), channel_id=1, source_target_pairs={{0,1},{1,2},{2,3},{3,4},{4,5},{5,6},{6,7},{8,9},{9,10},{10,11},{11... | collective-permute-start | bytes 786440 | tf_op jit(solution)/shard_map/ppermute | solution.py:13
  36.9 14.1 %collective-permute-start.6 = (bf16[8,64,256]{2,1,0:T(8,128)(2,1)S(1)}, bf16[8,64,256]{2,1,0:T(8,128)(2,1)S(1)}, u32[]{:S(2)}, u32[]{:S(2)}) collective-permute-start(bf16[8,64,256]{2,1,0:T(8,128)(2,1)S(1)} %get-tuple-element.156), channel_id=1, source_target_pairs={{0,1},{1,2},{2,3},{3,4},{4,5},{5,6},{6,7},{8,9},{9,10},{10,11},{11... | collective-permute-start | bytes 786440 | tf_op jit(solution)/shard_map/ppermute | solution.py:13
  40.2 20.5 %collective-permute-start.9 = (bf16[8,64,256]{2,1,0:T(8,128)(2,1)S(1)}, bf16[8,64,256]{2,1,0:T(8,128)(2,1)S(1)}, u32[]{:S(2)}, u32[]{:S(2)}) collective-permute-start(bf16[8,64,256]{2,1,0:T(8,128)(2,1)S(1)} %get-tuple-element.154), channel_id=1, source_target_pairs={{0,8},{8,16},{16,24},{24,32},{32,40},{40,48},{48,56},{56,64},{64,7... | collective-permute-start | bytes 786440 | tf_op jit(solution)/shard_map/ppermute | solution.py:13
  44.2 10.5 %collective-permute-start.8 = (bf16[8,64,256]{2,1,0:T(8,128)(2,1)S(1)}, bf16[8,64,256]{2,1,0:T(8,128)(2,1)S(1)}, u32[]{:S(2)}, u32[]{:S(2)}) collective-permute-start(bf16[8,64,256]{2,1,0:T(8,128)(2,1)S(1)} %collective-permute-done.7), channel_id=1, source_target_pairs={{1,0},{2,1},{3,2},{4,3},{5,4},{6,5},{7,6},{9,8},{10,9},{11,10},{12... | collective-permute-start | bytes 786440 | tf_op jit(solution)/shard_map/ppermute | solution.py:13
  45.5 15.2 %collective-permute-start.11 = (bf16[8,64,256]{2,1,0:T(8,128)(2,1)S(1)}, bf16[8,64,256]{2,1,0:T(8,128)(2,1)S(1)}, u32[]{:S(2)}, u32[]{:S(2)}) collective-permute-start(bf16[8,64,256]{2,1,0:T(8,128)(2,1)S(1)} %collective-permute-done.10), channel_id=1, source_target_pairs={{0,1},{1,2},{2,3},{3,4},{4,5},{5,6},{6,7},{8,9},{9,10},{10,11},{11... | collective-permute-start | bytes 786440 | tf_op jit(solution)/shard_map/ppermute | solution.py:13
  837.1 3.2 copy-start.6
  837.1 9.8 copy-start.1
  838.2 6.7 collective-permute-start.12
  840.3 20.3 %collective-permute-start.14 = (bf16[8,64,256]{2,1,0:T(8,128)(2,1)}, bf16[8,64,256]{2,1,0:T(8,128)(2,1)S(1)}, u32[]{:S(2)}, u32[]{:S(2)}) collective-permute-start(bf16[8,64,256]{2,1,0:T(8,128)(2,1)} %get-tuple-element.149), channel_id=1, source_target_pairs={{0,8},{8,16},{16,24},{24,32},{32,40},{40,48},{48,56},{56,64},{64,7... | collective-permute-start | bytes 786440 | tf_op jit(solution)/shard_map/ppermute | solution.py:13
  842.2 6.5 copy-start.3
  842.3 10.5 %copy-start.5 = (bf16[8,64,256]{2,1,0:T(8,128)(2,1)S(1)}, bf16[8,64,256]{2,1,0:T(8,128)(2,1)}, u32[]{:S(2)}) copy-start(bf16[8,64,256]{2,1,0:T(8,128)(2,1)} %get-tuple-element.145) | copy-start | bytes 786436
  842.3 12.7 %copy-start.4 = (bf16[8,64,256]{2,1,0:T(8,128)(2,1)S(1)}, bf16[8,64,256]{2,1,0:T(8,128)(2,1)}, u32[]{:S(2)}) copy-start(bf16[8,64,256]{2,1,0:T(8,128)(2,1)} %get-tuple-element.143) | copy-start | bytes 786436
  842.3 18.4 %copy-start.2 = (bf16[8,64,256]{2,1,0:T(8,128)(2,1)S(1)}, bf16[8,64,256]{2,1,0:T(8,128)(2,1)}, u32[]{:S(2)}) copy-start(bf16[8,64,256]{2,1,0:T(8,128)(2,1)} %get-tuple-element.146) | copy-start | bytes 786436
  842.3 12.6 %collective-permute-start.15 = (bf16[8,64,256]{2,1,0:T(8,128)(2,1)}, bf16[8,64,256]{2,1,0:T(8,128)(2,1)S(1)}, u32[]{:S(2)}, u32[]{:S(2)}) collective-permute-start(bf16[8,64,256]{2,1,0:T(8,128)(2,1)} %get-tuple-element.148), channel_id=1, source_target_pairs={{1,0},{2,1},{3,2},{4,3},{5,4},{6,5},{7,6},{9,8},{10,9},{11,10},{12... | collective-permute-start | bytes 786440 | tf_op jit(solution)/shard_map/ppermute | solution.py:13
  844.9 11.3 %collective-permute-start.13 = (bf16[8,64,256]{2,1,0:T(8,128)(2,1)}, bf16[8,64,256]{2,1,0:T(8,128)(2,1)S(1)}, u32[]{:S(2)}, u32[]{:S(2)}) collective-permute-start(bf16[8,64,256]{2,1,0:T(8,128)(2,1)} %collective-permute-done.12), channel_id=1, source_target_pairs={{0,8},{8,16},{16,24},{24,32},{32,40},{40,48},{48,56},{56,64},{64,7... | collective-permute-start | bytes 786440 | tf_op jit(solution)/shard_map/ppermute | solution.py:13
  848.8 28.7 %collective-permute-start.17 = (bf16[8,64,256]{2,1,0:T(8,128)(2,1)S(1)}, bf16[8,64,256]{2,1,0:T(8,128)(2,1)S(1)}, u32[]{:S(2)}, u32[]{:S(2)}) collective-permute-start(bf16[8,64,256]{2,1,0:T(8,128)(2,1)S(1)} %copy-done.3), channel_id=1, source_target_pairs={{0,1},{1,2},{2,3},{3,4},{4,5},{5,6},{6,7},{8,9},{9,10},{10,11},{11... | collective-permute-start | bytes 786440 | tf_op jit(solution)/shard_map/ppermute | solution.py:13
  852.7 16.1 %collective-permute-start.19 = (bf16[8,64,256]{2,1,0:T(8,128)(2,1)S(1)}, bf16[8,64,256]{2,1,0:T(8,128)(2,1)S(1)}, u32[]{:S(2)}, u32[]{:S(2)}) collective-permute-start(bf16[8,64,256]{2,1,0:T(8,128)(2,1)S(1)} %copy-done.5), channel_id=1, source_target_pairs={{0,1},{1,2},{2,3},{3,4},{4,5},{5,6},{6,7},{8,9},{9,10},{10,11},{11... | collective-permute-start | bytes 786440 | tf_op jit(solution)/shard_map/ppermute | solution.py:13
  854.9 17.3 %collective-permute-start.22 = (bf16[8,64,256]{2,1,0:T(8,128)(2,1)S(1)}, bf16[8,64,256]{2,1,0:T(8,128)(2,1)S(1)}, u32[]{:S(2)}, u32[]{:S(2)}) collective-permute-start(bf16[8,64,256]{2,1,0:T(8,128)(2,1)S(1)} %copy-done.4), channel_id=1, source_target_pairs={{1,0},{2,1},{3,2},{4,3},{5,4},{6,5},{7,6},{9,8},{10,9},{11,10},{12... | collective-permute-start | bytes 786440 | tf_op jit(solution)/shard_map/ppermute | solution.py:13
  856.2 19.3 %collective-permute-start.16 = (bf16[8,64,256]{2,1,0:T(8,128)(2,1)S(1)}, bf16[8,64,256]{2,1,0:T(8,128)(2,1)S(1)}, u32[]{:S(2)}, u32[]{:S(2)}) collective-permute-start(bf16[8,64,256]{2,1,0:T(8,128)(2,1)S(1)} %collective-permute-done.15), channel_id=1, source_target_pairs={{0,8},{8,16},{16,24},{24,32},{32,40},{40,48},{48,56},{56,64},{64,7... | collective-permute-start | bytes 786440 | tf_op jit(solution)/shard_map/ppermute | solution.py:13
  860.6 19.3 %collective-permute-start.18 = (bf16[8,64,256]{2,1,0:T(8,128)(2,1)S(1)}, bf16[8,64,256]{2,1,0:T(8,128)(2,1)S(1)}, u32[]{:S(2)}, u32[]{:S(2)}) collective-permute-start(bf16[8,64,256]{2,1,0:T(8,128)(2,1)S(1)} %copy-done.2), channel_id=1, source_target_pairs={{1,0},{2,1},{3,2},{4,3},{5,4},{6,5},{7,6},{9,8},{10,9},{11,10},{12... | collective-permute-start | bytes 786440 | tf_op jit(solution)/shard_map/ppermute | solution.py:13
  868.8 19.9 %collective-permute-start.21 = (bf16[8,64,256]{2,1,0:T(8,128)(2,1)S(1)}, bf16[8,64,256]{2,1,0:T(8,128)(2,1)S(1)}, u32[]{:S(2)}, u32[]{:S(2)}) collective-permute-start(bf16[8,64,256]{2,1,0:T(8,128)(2,1)S(1)} %get-tuple-element.144), channel_id=1, source_target_pairs={{8,0},{16,8},{24,16},{32,24},{40,32},{48,40},{56,48},{64,56},{72,6... | collective-permute-start | bytes 786440 | tf_op jit(solution)/shard_map/ppermute | solution.py:13
  872.3 16.4 %collective-permute-start.20 = (bf16[8,64,256]{2,1,0:T(8,128)(2,1)S(1)}, bf16[8,64,256]{2,1,0:T(8,128)(2,1)S(1)}, u32[]{:S(2)}, u32[]{:S(2)}) collective-permute-start(bf16[8,64,256]{2,1,0:T(8,128)(2,1)S(1)} %collective-permute-done.19), channel_id=1, source_target_pairs={{8,0},{16,8},{24,16},{32,24},{40,32},{48,40},{56,48},{64,56},{72,6... | collective-permute-start | bytes 786440 | tf_op jit(solution)/shard_map/ppermute | solution.py:13
  875.5 16.0 %collective-permute-start.23 = (bf16[8,64,256]{2,1,0:T(8,128)(2,1)S(1)}, bf16[8,64,256]{2,1,0:T(8,128)(2,1)S(1)}, u32[]{:S(2)}, u32[]{:S(2)}) collective-permute-start(bf16[8,64,256]{2,1,0:T(8,128)(2,1)S(1)} %collective-permute-done.22), channel_id=1, source_target_pairs={{8,0},{16,8},{24,16},{32,24},{40,32},{48,40},{56,48},{64,56},{72,6... | collective-permute-start | bytes 786440 | tf_op jit(solution)/shard_map/ppermute | solution.py:13
Sparse Core Ops, SparseCore 0:
  833.9 177.0 all-reduce.5
where the time goes:
time: 1030 us; the launch traced here: 1020 us
  other arithmetic  412 us (40%)
  local copies, waits for them, and re-layouts  223 us (22%)
  matrix products  167 us (16%)
  waiting for transfers between devices  142 us (14%)
  starting transfers between devices  63.9 us (6%)
  between operations  15.4 us (1%)
    scatter-add x14, other arithmetic, backward_turn(): ext_grad.at[turn_inputs.reshape(-1)]  190 us
    scatter-add x14, other arithmetic, forward_turn(): accum.at[turn_outputs.reshape(-1)]  123 us
    psum x1, waiting for transfers between devices, shards(): weight_total = lax.psum(weight_part, ('gx', 'gy'))  107 us
    scatter-add x14, other arithmetic, backward_turn(): weight_part = weight_part.at[turn_offsets].add(terms)  65.3 us
    ppermute x24, starting transfers between devices, passed_along(): return lax.ppermute(x, axis, pairs)  63.8 us
    dot_general x14, matrix products, forward_turn(): jnp.einsum('grc,gcd->grd', gathered, weights[turn_offsets], preferred_ele...  60.4 us
    dot_general x14, matrix products, backward_turn(): jnp.einsum('grd,gcd->grc', grads, mats, preferred_element_type=jnp.float32)  55 us
    gather x14, local copies, waits for them, and re-layouts, forward_turn(): extended[turn_inputs.reshape(-1)]  54.7 us
  transfers between devices with their start and end apart: 25, of which 9 were waited for; matrix products, arithmetic and copies ran while one was open for 2% of the time, Pallas kernels for 0%

commit v1 on v0

--- a/solution.py
+++ b/solution.py
@@ -117,7 +117,7 @@
     feat_sum = incoming + ext_grad[:tile_slots]
     feat_sum = feat_sum.at[lists.reshape(-1)].add(returned.reshape(8 * halo_size, voxels, channels))
     feat_grad = feat_sum.astype(jnp.bfloat16)
-    weight_total = lax.psum(weight_part, ("gx", "gy"))
+    weight_total = lax.psum(lax.psum(weight_part, "gy"), "gx")
     device_total = lax.axis_size("gx") * lax.axis_size("gy")
     weight_grad = weight_total / math.sqrt(voxels * tile_slots * device_total)
     return (out_features[None, None], feat_grad[None, None], weight_grad)

time: 1030 us -> 1220 us (1.18)
  waiting for transfers between devices: 142 us -> 325 us
    psum x1 -> x2, waiting for transfers between devices: 107 us -> 268 us  [shards(): weight_total = lax.psum(lax.psum(weight_part, 'gy'), 'gx')]
    ppermute x24, waiting for transfers between devices: 35.3 us -> 57.2 us  [passed_along(): return lax.ppermute(x, axis, pairs)]
  transfers between devices with their start and end apart: 25 -> 26, of which waited for: 9 -> 9; matrix products, arithmetic and copies ran while one was open for 2% -> 2% of each run, Pallas kernels for 0% -> 0%
where the time goes in v1:
time: 1220 us; the launch traced here: 1210 us
  other arithmetic  412 us (34%)
  waiting for transfers between devices  325 us (27%)
  local copies, waits for them, and re-layouts  223 us (18%)
  matrix products  167 us (14%)
  starting transfers between devices  68.3 us (6%)
  between operations  15.4 us (1%)
    psum x2, waiting for transfers between devices, shards(): weight_total = lax.psum(lax.psum(weight_part, 'gy'), 'gx')  268 us
    scatter-add x14, other arithmetic, backward_turn(): ext_grad.at[turn_inputs.reshape(-1)]  190 us
    scatter-add x14, other arithmetic, forward_turn(): accum.at[turn_outputs.reshape(-1)]  123 us
    ppermute x24, starting transfers between devices, passed_along(): return lax.ppermute(x, axis, pairs)  68.2 us
    scatter-add x14, other arithmetic, backward_turn(): weight_part = weight_part.at[turn_offsets].add(terms)  65.2 us
    dot_general x14, matrix products, forward_turn(): jnp.einsum('grc,gcd->grd', gathered, weights[turn_offsets], preferred_ele...  60.4 us
    ppermute x24, waiting for transfers between devices, passed_along(): return lax.ppermute(x, axis, pairs)  57.2 us
    dot_general x14, matrix products, backward_turn(): jnp.einsum('grd,gcd->grc', grads, mats, preferred_element_type=jnp.float32)  55 us
  transfers between devices with their start and end apart: 26, of which 9 were waited for; matrix products, arithmetic and copies ran while one was open for 2% of the time, Pallas kernels for 0%

profile of v1, /device:TPU:1, one launch (start us, length us, event | category | flops | bytes accessed | tf_op | source)
XLA Modules:
  0.0 1211.7 jit_solution(3663239895401281881)
XLA Ops:
  19.4 5.1 collective-permute-start.7
  45.5 5.5 collective-permute-start.11
  54.7 5.9 collective-permute-done.9
  62.9 279.6 %while.22 = (s32[]{:T(128)}, f32[32,64,256]{2,1,0:T(8,128)S(1)}, s32[]{:T(128)}, s32[112,8]{1,0:T(8,128)S(1)}, s32[112,8]{1,0:T(8,128)S(1)}, /*index=5*/bf16[96,...) while((s32[]{:T(128)}, f32[32,64,256]{2,1,0:T(8,128)S(1)}, ...), condition=%wide.region_2.3_spmd, body=%wide.region_0.2_spmd.sunk | while | flops 537921920 | bytes 26226740 | solution.py:79
  74.1 8.8 scatter_fusion
  94.0 8.8 scatter_fusion
  114.0 8.8 scatter_fusion
  134.0 8.8 scatter_fusion
  153.9 8.8 scatter_fusion
  173.9 8.8 scatter_fusion
  193.9 8.8 scatter_fusion
  213.9 8.8 scatter_fusion
  233.8 8.8 scatter_fusion
  253.8 8.8 scatter_fusion
  273.8 8.8 scatter_fusion
  293.7 8.8 scatter_fusion
  313.7 8.8 scatter_fusion
  333.7 8.8 scatter_fusion
  353.4 480.0 %while.23 = (s32[]{:T(128)}, f32[96,64,256]{2,1,0:T(8,128)}, f32[27,256,256]{2,1,0:T(8,128)}, s32[]{:T(128)}, s32[112,8]{1,0:T(8,128)S(1)}, /*index=5*/s32[112,8...) while((s32[]{:T(128)}, f32[96,64,256]{2,1,0:T(8,128)}, ...), condition=%wide.region_6.7_spmd, body=%wide.region_3.6_spmd.sunk | while | flops 1075318144 | bytes 43008608 | solution.py:112
  361.8 13.5 %scatter_fusion.1 = f32[96,64,256]{2,1,0:T(8,128)} fusion(f32[96,64,256]{2,1,0:T(8,128)} %get-tuple-element.332, s32[64]{0:T(128)S(1)} %fusion.41, f32[64,64,256]{2,1,0:T(8,128)} %bitcast.112), kind=kCustom, calls=%fused_computation.7.clone.1 | custom fusion | flops 1048576 | bytes 12583168 | tf_op jit(solution)/shard_map/while/body/scatter-add | solution.py:101
  382.9 4.7 scatter_fusion.2
  396.1 13.5 %scatter_fusion.1 = f32[96,64,256]{2,1,0:T(8,128)} fusion(f32[96,64,256]{2,1,0:T(8,128)} %get-tuple-element.332, s32[64]{0:T(128)S(1)} %fusion.41, f32[64,64,256]{2,1,0:T(8,128)} %bitcast.112), kind=kCustom, calls=%fused_computation.7.clone.1 | custom fusion | flops 1048576 | bytes 12583168 | tf_op jit(solution)/shard_map/while/body/scatter-add | solution.py:101
  417.2 4.8 scatter_fusion.2
  430.5 13.5 %scatter_fusion.1 = f32[96,64,256]{2,1,0:T(8,128)} fusion(f32[96,64,256]{2,1,0:T(8,128)} %get-tuple-element.332, s32[64]{0:T(128)S(1)} %fusion.41, f32[64,64,256]{2,1,0:T(8,128)} %bitcast.112), kind=kCustom, calls=%fused_computation.7.clone.1 | custom fusion | flops 1048576 | bytes 12583168 | tf_op jit(solution)/shard_map/while/body/scatter-add | solution.py:101
  464.6 13.5 %scatter_fusion.1 = f32[96,64,256]{2,1,0:T(8,128)} fusion(f32[96,64,256]{2,1,0:T(8,128)} %get-tuple-element.332, s32[64]{0:T(128)S(1)} %fusion.41, f32[64,64,256]{2,1,0:T(8,128)} %bitcast.112), kind=kCustom, calls=%fused_computation.7.clone.1 | custom fusion | flops 1048576 | bytes 12583168 | tf_op jit(solution)/shard_map/while/body/scatter-add | solution.py:101
  498.8 13.4 %scatter_fusion.1 = f32[96,64,256]{2,1,0:T(8,128)} fusion(f32[96,64,256]{2,1,0:T(8,128)} %get-tuple-element.332, s32[64]{0:T(128)S(1)} %fusion.41, f32[64,64,256]{2,1,0:T(8,128)} %bitcast.112), kind=kCustom, calls=%fused_computation.7.clone.1 | custom fusion | flops 1048576 | bytes 12583168 | tf_op jit(solution)/shard_map/while/body/scatter-add | solution.py:101
  533.0 13.4 %scatter_fusion.1 = f32[96,64,256]{2,1,0:T(8,128)} fusion(f32[96,64,256]{2,1,0:T(8,128)} %get-tuple-element.332, s32[64]{0:T(128)S(1)} %fusion.41, f32[64,64,256]{2,1,0:T(8,128)} %bitcast.112), kind=kCustom, calls=%fused_computation.7.clone.1 | custom fusion | flops 1048576 | bytes 12583168 | tf_op jit(solution)/shard_map/while/body/scatter-add | solution.py:101
  554.0 4.7 scatter_fusion.2
  567.2 13.4 %scatter_fusion.1 = f32[96,64,256]{2,1,0:T(8,128)} fusion(f32[96,64,256]{2,1,0:T(8,128)} %get-tuple-element.332, s32[64]{0:T(128)S(1)} %fusion.41, f32[64,64,256]{2,1,0:T(8,128)} %bitcast.112), kind=kCustom, calls=%fused_computation.7.clone.1 | custom fusion | flops 1048576 | bytes 12583168 | tf_op jit(solution)/shard_map/while/body/scatter-add | solution.py:101
  601.3 13.6 %scatter_fusion.1 = f32[96,64,256]{2,1,0:T(8,128)} fusion(f32[96,64,256]{2,1,0:T(8,128)} %get-tuple-element.332, s32[64]{0:T(128)S(1)} %fusion.41, f32[64,64,256]{2,1,0:T(8,128)} %bitcast.112), kind=kCustom, calls=%fused_computation.7.clone.1 | custom fusion | flops 1048576 | bytes 12583168 | tf_op jit(solution)/shard_map/while/body/scatter-add | solution.py:101
  635.6 13.5 %scatter_fusion.1 = f32[96,64,256]{2,1,0:T(8,128)} fusion(f32[96,64,256]{2,1,0:T(8,128)} %get-tuple-element.332, s32[64]{0:T(128)S(1)} %fusion.41, f32[64,64,256]{2,1,0:T(8,128)} %bitcast.112), kind=kCustom, calls=%fused_computation.7.clone.1 | custom fusion | flops 1048576 | bytes 12583168 | tf_op jit(solution)/shard_map/while/body/scatter-add | solution.py:101
  656.7 4.7 scatter_fusion.2
  669.9 13.6 %scatter_fusion.1 = f32[96,64,256]{2,1,0:T(8,128)} fusion(f32[96,64,256]{2,1,0:T(8,128)} %get-tuple-element.332, s32[64]{0:T(128)S(1)} %fusion.41, f32[64,64,256]{2,1,0:T(8,128)} %bitcast.112), kind=kCustom, calls=%fused_computation.7.clone.1 | custom fusion | flops 1048576 | bytes 12583168 | tf_op jit(solution)/shard_map/while/body/scatter-add | solution.py:101
  691.1 4.7 scatter_fusion.2
  704.2 13.6 %scatter_fusion.1 = f32[96,64,256]{2,1,0:T(8,128)} fusion(f32[96,64,256]{2,1,0:T(8,128)} %get-tuple-element.332, s32[64]{0:T(128)S(1)} %fusion.41, f32[64,64,256]{2,1,0:T(8,128)} %bitcast.112), kind=kCustom, calls=%fused_computation.7.clone.1 | custom fusion | flops 1048576 | bytes 12583168 | tf_op jit(solution)/shard_map/while/body/scatter-add | solution.py:101
  738.5 13.6 %scatter_fusion.1 = f32[96,64,256]{2,1,0:T(8,128)} fusion(f32[96,64,256]{2,1,0:T(8,128)} %get-tuple-element.332, s32[64]{0:T(128)S(1)} %fusion.41, f32[64,64,256]{2,1,0:T(8,128)} %bitcast.112), kind=kCustom, calls=%fused_computation.7.clone.1 | custom fusion | flops 1048576 | bytes 12583168 | tf_op jit(solution)/shard_map/while/body/scatter-add | solution.py:101
  772.7 13.6 %scatter_fusion.1 = f32[96,64,256]{2,1,0:T(8,128)} fusion(f32[96,64,256]{2,1,0:T(8,128)} %get-tuple-element.332, s32[64]{0:T(128)S(1)} %fusion.41, f32[64,64,256]{2,1,0:T(8,128)} %bitcast.112), kind=kCustom, calls=%fused_computation.7.clone.1 | custom fusion | flops 1048576 | bytes 12583168 | tf_op jit(solution)/shard_map/while/body/scatter-add | solution.py:101
  807.0 14.0 %scatter_fusion.1 = f32[96,64,256]{2,1,0:T(8,128)} fusion(f32[96,64,256]{2,1,0:T(8,128)} %get-tuple-element.332, s32[64]{0:T(128)S(1)} %fusion.41, f32[64,64,256]{2,1,0:T(8,128)} %bitcast.112), kind=kCustom, calls=%fused_computation.7.clone.1 | custom fusion | flops 1048576 | bytes 12583168 | tf_op jit(solution)/shard_map/while/body/scatter-add | solution.py:101
  828.6 4.8 scatter_fusion.2
  833.5 162.7 %all-reduce.7.cloned.1.call-done = f32[27,256,256]{2,1,0:T(8,128)} async-done(((f32[27,256,256]{2,1,0:T(8,128)}), f32[27,256,256]{2,1,0:T(8,128)}) %all-reduce.7.cloned.1.call-update) | async-done | bytes 7077904 | tf_op jit(solution)/shard_map/psum | solution.py:120
  1002.7 5.4 collective-permute-start.14
  1023.0 15.7 %collective-permute-done.13 = bf16[8,64,256]{2,1,0:T(8,128)(2,1)S(1)} collective-permute-done((bf16[8,64,256]{2,1,0:T(8,128)(2,1)}, bf16[8,64,256]{2,1,0:T(8,128)(2,1)S(1)}, u32[]{:S(2)}, u32[]{:S(2)}) %collective-permute-start.13) | collective-permute-done | bytes 262176 | tf_op jit(solution)/shard_map/ppermute | solution.py:13
  1038.7 6.0 collective-permute-start.16
  1055.1 16.5 %collective-permute-done.20 = bf16[8,64,256]{2,1,0:T(8,128)(2,1)S(1)} collective-permute-done((bf16[8,64,256]{2,1,0:T(8,128)(2,1)S(1)}, bf16[8,64,256]{2,1,0:T(8,128)(2,1)S(1)}, u32[]{:S(2)}, u32[]{:S(2)}) %collective-permute-start.20) | collective-permute-done | bytes 262176 | tf_op jit(solution)/shard_map/ppermute | solution.py:13
  1071.7 8.4 collective-permute-done.23
  1082.8 8.9 scatter_fusion.3
  1092.8 105.4 %all-reduce.9.cloned.1.call-done = f32[27,256,256]{2,1,0:T(8,128)} async-done(((f32[27,256,256]{2,1,0:T(8,128)}), f32[27,256,256]{2,1,0:T(8,128)}) %all-reduce.9.cloned.1.call-update) | async-done | bytes 7077904 | tf_op jit(solution)/shard_map/psum | solution.py:120
  1198.2 6.7 broadcast_multiply_fusion
  (462 shorter events, 501.9 us)
Async XLA Ops:
  7.2 989.0 %all-reduce.7.cloned.1.call-start = ((), (), s32[]{:S(2)}) async-start(), calls=%async_computation | async-start | bytes 14155776 | tf_op jit(solution)/shard_map/psum | solution.py:120
  9.9 16.6 %copy-start.7 = (s32[1,1,108,8]{2,3,1,0:T(8,128)S(1)}, s32[1,1,108,8]{2,3,1,0:T(8,128)}, u32[]{:S(2)}) copy-start(s32[1,1,108,8]{2,3,1,0:T(8,128)} %param.18) | copy-start | bytes 10372
  9.9 16.8 %copy-start.8 = (s32[1,1,108,8]{2,3,1,0:T(8,128)S(1)}, s32[1,1,108,8]{2,3,1,0:T(8,128)}, u32[]{:S(2)}) copy-start(s32[1,1,108,8]{2,3,1,0:T(8,128)} %param.17) | copy-start | bytes 10372
  9.9 17.0 %copy-start.9 = (s32[1,1,108]{2,1,0:T(1,128)S(1)}, s32[1,1,108]{2,1,0:T(1,128)}, u32[]{:S(2)}) copy-start(s32[1,1,108]{2,1,0:T(1,128)} %param.16) | copy-start | bytes 1300
  11.0 14.2 %collective-permute-start = (bf16[8,64,256]{2,1,0:T(8,128)(2,1)S(1)}, bf16[8,64,256]{2,1,0:T(8,128)(2,1)S(1)}, u32[]{:S(2)}, u32[]{:S(2)}) collective-permute-start(bf16[8,64,256]{2,1,0:T(8,128)(2,1)S(1)} %get-tuple-element.160), channel_id=1, source_target_pairs={{8,0},{16,8},{24,16},{32,24},{40,32},{48,40},{56,48},{64,56},{72,6... | collective-permute-start | bytes 786440 | tf_op jit(solution)/shard_map/ppermute | solution.py:13
  14.2 22.7 %collective-permute-start.2 = (bf16[8,64,256]{2,1,0:T(8,128)(2,1)}, bf16[8,64,256]{2,1,0:T(8,128)(2,1)S(1)}, u32[]{:S(2)}, u32[]{:S(2)}) collective-permute-start(bf16[8,64,256]{2,1,0:T(8,128)(2,1)} %get-tuple-element.159), channel_id=1, source_target_pairs={{8,0},{16,8},{24,16},{32,24},{40,32},{48,40},{56,48},{64,56},{72,6... | collective-permute-start | bytes 786440 | tf_op jit(solution)/shard_map/ppermute | solution.py:13
  16.2 10.7 collective-permute-start.3
  18.1 32.9 %collective-permute-start.5 = (bf16[8,64,256]{2,1,0:T(8,128)(2,1)S(1)}, bf16[8,64,256]{2,1,0:T(8,128)(2,1)S(1)}, u32[]{:S(2)}, u32[]{:S(2)}) collective-permute-start(bf16[8,64,256]{2,1,0:T(8,128)(2,1)S(1)} %get-tuple-element.157), channel_id=1, source_target_pairs={{1,0},{2,1},{3,2},{4,3},{5,4},{6,5},{7,6},{9,8},{10,9},{11,10},{12... | collective-permute-start | bytes 786440 | tf_op jit(solution)/shard_map/ppermute | solution.py:13
  19.4 20.8 %collective-permute-start.7 = (bf16[8,64,256]{2,1,0:T(8,128)(2,1)S(1)}, bf16[8,64,256]{2,1,0:T(8,128)(2,1)S(1)}, u32[]{:S(2)}, u32[]{:S(2)}) collective-permute-start(bf16[8,64,256]{2,1,0:T(8,128)(2,1)S(1)} %get-tuple-element.155), channel_id=1, source_target_pairs={{0,8},{8,16},{16,24},{24,32},{32,40},{40,48},{48,56},{56,64},{64,7... | collective-permute-start | bytes 786440 | tf_op jit(solution)/shard_map/ppermute | solution.py:13
  25.2 8.0 collective-permute-start.1
  26.9 33.8 %copy-start = (bf16[1,1,32,64,256]{4,3,2,1,0:T(8,128)(2,1)S(1)}, bf16[1,1,32,64,256]{4,3,2,1,0:T(8,128)(2,1)}, u32[]{:S(2)}) copy-start(bf16[1,1,32,64,256]{4,3,2,1,0:T(8,128)(2,1)} %param.12) | copy-start | bytes 3145732
  26.9 17.2 %collective-permute-start.10 = (bf16[8,64,256]{2,1,0:T(8,128)(2,1)S(1)}, bf16[8,64,256]{2,1,0:T(8,128)(2,1)S(1)}, u32[]{:S(2)}, u32[]{:S(2)}) collective-permute-start(bf16[8,64,256]{2,1,0:T(8,128)(2,1)S(1)} %get-tuple-element.153), channel_id=1, source_target_pairs={{0,8},{8,16},{16,24},{24,32},{32,40},{40,48},{48,56},{56,64},{64,7... | collective-permute-start | bytes 786440 | tf_op jit(solution)/shard_map/ppermute | solution.py:13
  33.2 12.2 %collective-permute-start.4 = (bf16[8,64,256]{2,1,0:T(8,128)(2,1)S(1)}, bf16[8,64,256]{2,1,0:T(8,128)(2,1)S(1)}, u32[]{:S(2)}, u32[]{:S(2)}) collective-permute-start(bf16[8,64,256]{2,1,0:T(8,128)(2,1)S(1)} %collective-permute-done.3), channel_id=1, source_target_pairs={{0,1},{1,2},{2,3},{3,4},{4,5},{5,6},{6,7},{8,9},{9,10},{10,11},{11... | collective-permute-start | bytes 786440 | tf_op jit(solution)/shard_map/ppermute | solution.py:13
  36.9 14.1 %collective-permute-start.6 = (bf16[8,64,256]{2,1,0:T(8,128)(2,1)S(1)}, bf16[8,64,256]{2,1,0:T(8,128)(2,1)S(1)}, u32[]{:S(2)}, u32[]{:S(2)}) collective-permute-start(bf16[8,64,256]{2,1,0:T(8,128)(2,1)S(1)} %get-tuple-element.156), channel_id=1, source_target_pairs={{0,1},{1,2},{2,3},{3,4},{4,5},{5,6},{6,7},{8,9},{9,10},{10,11},{11... | collective-permute-start | bytes 786440 | tf_op jit(solution)/shard_map/ppermute | solution.py:13
  40.2 20.5 %collective-permute-start.9 = (bf16[8,64,256]{2,1,0:T(8,128)(2,1)S(1)}, bf16[8,64,256]{2,1,0:T(8,128)(2,1)S(1)}, u32[]{:S(2)}, u32[]{:S(2)}) collective-permute-start(bf16[8,64,256]{2,1,0:T(8,128)(2,1)S(1)} %get-tuple-element.154), channel_id=1, source_target_pairs={{0,8},{8,16},{16,24},{24,32},{32,40},{40,48},{48,56},{56,64},{64,7... | collective-permute-start | bytes 786440 | tf_op jit(solution)/shard_map/ppermute | solution.py:13
  44.2 10.5 collective-permute-start.8
  45.5 15.2 %collective-permute-start.11 = (bf16[8,64,256]{2,1,0:T(8,128)(2,1)S(1)}, bf16[8,64,256]{2,1,0:T(8,128)(2,1)S(1)}, u32[]{:S(2)}, u32[]{:S(2)}) collective-permute-start(bf16[8,64,256]{2,1,0:T(8,128)(2,1)S(1)} %collective-permute-done.10), channel_id=1, source_target_pairs={{0,1},{1,2},{2,3},{3,4},{4,5},{5,6},{6,7},{8,9},{9,10},{10,11},{11... | collective-permute-start | bytes 786440 | tf_op jit(solution)/shard_map/ppermute | solution.py:13
  833.4 364.8 %all-reduce.9.cloned.1.call-start = ((), (), s32[]{:S(2)}) async-start(), calls=%async_computation.1 | async-start | bytes 14155776 | tf_op jit(solution)/shard_map/psum | solution.py:120
  999.4 3.2 copy-start.6
  999.5 13.2 %copy-start.1 = (bf16[1,1,32,64,256]{4,3,2,1,0:T(8,128)(2,1)S(1)}, bf16[1,1,32,64,256]{4,3,2,1,0:T(8,128)(2,1)}, u32[]{:S(2)}) copy-start(bf16[1,1,32,64,256]{4,3,2,1,0:T(8,128)(2,1)} %param.14) | copy-start | bytes 3145732
  1000.6 9.0 collective-permute-start.12
  1002.7 42.0 %collective-permute-start.14 = (bf16[8,64,256]{2,1,0:T(8,128)(2,1)}, bf16[8,64,256]{2,1,0:T(8,128)(2,1)S(1)}, u32[]{:S(2)}, u32[]{:S(2)}) collective-permute-start(bf16[8,64,256]{2,1,0:T(8,128)(2,1)} %get-tuple-element.149), channel_id=1, source_target_pairs={{0,8},{8,16},{16,24},{24,32},{32,40},{40,48},{48,56},{56,64},{64,7... | collective-permute-start | bytes 786440 | tf_op jit(solution)/shard_map/ppermute | solution.py:13
  1008.1 6.5 copy-start.3
  1008.1 10.7 copy-start.5
  1008.1 13.5 %copy-start.4 = (bf16[8,64,256]{2,1,0:T(8,128)(2,1)S(1)}, bf16[8,64,256]{2,1,0:T(8,128)(2,1)}, u32[]{:S(2)}) copy-start(bf16[8,64,256]{2,1,0:T(8,128)(2,1)} %get-tuple-element.143) | copy-start | bytes 786436
  1008.1 36.6 %copy-start.2 = (bf16[8,64,256]{2,1,0:T(8,128)(2,1)S(1)}, bf16[8,64,256]{2,1,0:T(8,128)(2,1)}, u32[]{:S(2)}) copy-start(bf16[8,64,256]{2,1,0:T(8,128)(2,1)} %get-tuple-element.146) | copy-start | bytes 786436
  1008.2 13.5 %collective-permute-start.15 = (bf16[8,64,256]{2,1,0:T(8,128)(2,1)}, bf16[8,64,256]{2,1,0:T(8,128)(2,1)S(1)}, u32[]{:S(2)}, u32[]{:S(2)}) collective-permute-start(bf16[8,64,256]{2,1,0:T(8,128)(2,1)} %get-tuple-element.148), channel_id=1, source_target_pairs={{1,0},{2,1},{3,2},{4,3},{5,4},{6,5},{7,6},{9,8},{10,9},{11,10},{12... | collective-permute-start | bytes 786440 | tf_op jit(solution)/shard_map/ppermute | solution.py:13
  1009.6 29.1 %collective-permute-start.13 = (bf16[8,64,256]{2,1,0:T(8,128)(2,1)}, bf16[8,64,256]{2,1,0:T(8,128)(2,1)S(1)}, u32[]{:S(2)}, u32[]{:S(2)}) collective-permute-start(bf16[8,64,256]{2,1,0:T(8,128)(2,1)} %collective-permute-done.12), channel_id=1, source_target_pairs={{0,8},{8,16},{16,24},{24,32},{32,40},{40,48},{48,56},{56,64},{64,7... | collective-permute-start | bytes 786440 | tf_op jit(solution)/shard_map/ppermute | solution.py:13
  1014.6 40.5 %collective-permute-start.17 = (bf16[8,64,256]{2,1,0:T(8,128)(2,1)S(1)}, bf16[8,64,256]{2,1,0:T(8,128)(2,1)S(1)}, u32[]{:S(2)}, u32[]{:S(2)}) collective-permute-start(bf16[8,64,256]{2,1,0:T(8,128)(2,1)S(1)} %copy-done.3), channel_id=1, source_target_pairs={{0,1},{1,2},{2,3},{3,4},{4,5},{5,6},{6,7},{8,9},{9,10},{10,11},{11... | collective-permute-start | bytes 786440 | tf_op jit(solution)/shard_map/ppermute | solution.py:13
  1018.9 27.2 %collective-permute-start.19 = (bf16[8,64,256]{2,1,0:T(8,128)(2,1)S(1)}, bf16[8,64,256]{2,1,0:T(8,128)(2,1)S(1)}, u32[]{:S(2)}, u32[]{:S(2)}) collective-permute-start(bf16[8,64,256]{2,1,0:T(8,128)(2,1)S(1)} %copy-done.5), channel_id=1, source_target_pairs={{0,1},{1,2},{2,3},{3,4},{4,5},{5,6},{6,7},{8,9},{9,10},{10,11},{11... | collective-permute-start | bytes 786440 | tf_op jit(solution)/shard_map/ppermute | solution.py:13
  1021.7 26.3 %collective-permute-start.22 = (bf16[8,64,256]{2,1,0:T(8,128)(2,1)S(1)}, bf16[8,64,256]{2,1,0:T(8,128)(2,1)S(1)}, u32[]{:S(2)}, u32[]{:S(2)}) collective-permute-start(bf16[8,64,256]{2,1,0:T(8,128)(2,1)S(1)} %copy-done.4), channel_id=1, source_target_pairs={{1,0},{2,1},{3,2},{4,3},{5,4},{6,5},{7,6},{9,8},{10,9},{11,10},{12... | collective-permute-start | bytes 786440 | tf_op jit(solution)/shard_map/ppermute | solution.py:13
  1038.7 14.4 %collective-permute-start.16 = (bf16[8,64,256]{2,1,0:T(8,128)(2,1)S(1)}, bf16[8,64,256]{2,1,0:T(8,128)(2,1)S(1)}, u32[]{:S(2)}, u32[]{:S(2)}) collective-permute-start(bf16[8,64,256]{2,1,0:T(8,128)(2,1)S(1)} %collective-permute-done.15), channel_id=1, source_target_pairs={{0,8},{8,16},{16,24},{24,32},{32,40},{40,48},{48,56},{56,64},{64,7... | collective-permute-start | bytes 786440 | tf_op jit(solution)/shard_map/ppermute | solution.py:13
  1044.7 10.4 collective-permute-start.18
  1046.1 25.6 %collective-permute-start.21 = (bf16[8,64,256]{2,1,0:T(8,128)(2,1)S(1)}, bf16[8,64,256]{2,1,0:T(8,128)(2,1)S(1)}, u32[]{:S(2)}, u32[]{:S(2)}) collective-permute-start(bf16[8,64,256]{2,1,0:T(8,128)(2,1)S(1)} %get-tuple-element.144), channel_id=1, source_target_pairs={{8,0},{16,8},{24,16},{32,24},{40,32},{48,40},{56,48},{64,56},{72,6... | collective-permute-start | bytes 786440 | tf_op jit(solution)/shard_map/ppermute | solution.py:13
  1048.0 23.6 %collective-permute-start.20 = (bf16[8,64,256]{2,1,0:T(8,128)(2,1)S(1)}, bf16[8,64,256]{2,1,0:T(8,128)(2,1)S(1)}, u32[]{:S(2)}, u32[]{:S(2)}) collective-permute-start(bf16[8,64,256]{2,1,0:T(8,128)(2,1)S(1)} %collective-permute-done.19), channel_id=1, source_target_pairs={{8,0},{16,8},{24,16},{32,24},{40,32},{48,40},{56,48},{64,56},{72,6... | collective-permute-start | bytes 786440 | tf_op jit(solution)/shard_map/ppermute | solution.py:13
  1053.1 26.9 %collective-permute-start.23 = (bf16[8,64,256]{2,1,0:T(8,128)(2,1)S(1)}, bf16[8,64,256]{2,1,0:T(8,128)(2,1)S(1)}, u32[]{:S(2)}, u32[]{:S(2)}) collective-permute-start(bf16[8,64,256]{2,1,0:T(8,128)(2,1)S(1)} %collective-permute-done.22), channel_id=1, source_target_pairs={{8,0},{16,8},{24,16},{32,24},{40,32},{48,40},{56,48},{64,56},{72,6... | collective-permute-start | bytes 786440 | tf_op jit(solution)/shard_map/ppermute | solution.py:13
Sparse Core Ops, SparseCore 0:
  833.5 162.5 all-reduce.6
  998.7 199.4 all-reduce.8
